TPU v7x, 128 devices: a whole 4x4x4 slice. The times are simulated.
128 devices in a mesh: sx: 8 (over y_hi, x), sy: 8 (over z, core), par: 2 (over y_lo).
Axes of the slice: x: 4, y: 4 (y_hi: 2, y_lo: 2; y = y_hi * 2 + y_lo), z: 4, core: 2. Of those that a mesh axis runs over, the one named last changes fastest.
Arguments:
- initial_state: float32 [64, 128, 128, 128], P('par', 'sx', 'sy'), may hold values from -6 to 6
- conductivity: float32 [64, 128, 128, 128], P('par', 'sx', 'sy'), may hold values from 0.1 to 1
- omega: bfloat16 [64, 64], replicated, may hold values from -0.75 to 0.75
- psi: bfloat16 [64, 128, 128, 128], P(None, 'sx', 'sy'), may hold values from -0.01171875 to 0.01171875
- range_prev: bfloat16 [64, 128, 128, 128], P('par', 'sx', 'sy'), may hold values from -3 to 3
- corange_prev: float32 [64, 64], P(None, 'par'), may hold values from -3 to 3
Outputs:
- final_state: float32 [64, 128, 128, 128], P('par', 'sx', 'sy')
- range_sketch: bfloat16 [64, 128, 128, 128], P('par', 'sx', 'sy')
- corange_sketch: float32 [64, 64], P(None, 'par')
All inputs are finite; a program needn't handle non-finite values.
Results may differ from a plain program's by a relative error of at most 0.0033.
Values may be sent and summed in bfloat16 or wider, within the bound.
A program may use at most 192 MiB of HBM per device.

v0:
```python
import jax
import jax.numpy as jnp
from jax import lax
from jax.sharding import PartitionSpec as P

STEPS = 4


def extended(block, sides, width):
    for axis, dim in sides:
        count = lax.axis_size(axis)
        forward = [(i, i + 1) for i in range(count - 1)]
        backward = [(target, source) for source, target in forward]
        low = lax.ppermute(
            lax.slice_in_dim(block, block.shape[dim] - width, None, axis=dim), axis, forward
        )
        high = lax.ppermute(lax.slice_in_dim(block, 0, width, axis=dim), axis, backward)
        block = jnp.concatenate([low, block, high], axis=dim)
    return block


def advance(field, kpad):
    center = field[:, 1:-1, 1:-1, :]
    kcen = kpad[:, 1:-1, 1:-1, :]
    width_x = center.shape[1]
    width_y = center.shape[2]
    zfield = jnp.pad(center, ((0, 0), (0, 0), (0, 0), (1, 1)))
    zcond = jnp.pad(kcen, ((0, 0), (0, 0), (0, 0), (1, 1)))
    length = center.shape[3]
    pairs = [
        (field[:, 2:, 1:-1, :], kpad[:, 2:, 1:-1, :]),
        (field[:, :width_x, 1:-1, :], kpad[:, :width_x, 1:-1, :]),
        (field[:, 1:-1, 2:, :], kpad[:, 1:-1, 2:, :]),
        (field[:, 1:-1, :width_y, :], kpad[:, 1:-1, :width_y, :]),
        (zfield[:, :, :, 2:], zcond[:, :, :, 2:]),
        (zfield[:, :, :, :length], zcond[:, :, :, :length]),
    ]
    total = jnp.zeros_like(center)
    for unb, knb in pairs:
        total = total + 0.5 * (kcen + knb) * (unb - center)
    return center + 0.16 * total


def per_device(initial_state, conductivity, omega, psi, range_prev, corange_prev):
    samples, cells_x, cells_y, length = initial_state.shape
    kpad = extended(conductivity, (("sx", 1), ("sy", 2)), 1)
    state = initial_state
    for step in range(STEPS):
        field = extended(state, (("sx", 1), ("sy", 2)), 1)
        state = advance(field, kpad)
    snapshot = state.astype(jnp.bfloat16)
    flat_snap = snapshot.reshape(samples, cells_x * cells_y * length)
    rank = omega.shape[1]
    rank_dev = range_prev.shape[0]
    own_cols = lax.dynamic_slice_in_dim(omega, lax.axis_index("par") * rank_dev, rank_dev, 1)
    start_sum = range_prev.astype(jnp.float32)
    piece = lax.all_gather(snapshot, "par", axis=0, tiled=True)
    rows = piece.shape[0]
    term = lax.dot_general(
        own_cols,
        piece.reshape(rows, -1),
        (((0,), (0,)), ((), ())),
        preferred_element_type=jnp.float32,
    )
    range_sum = start_sum + term.reshape(start_sum.shape)
    range_sketch = range_sum.astype(jnp.bfloat16)
    flat_psi = psi.reshape(rank, cells_x * cells_y * length)
    partial_value = lax.dot_general(
        flat_psi, flat_snap, (((1,), (1,)), ((), ())), preferred_element_type=jnp.float32
    )
    corange_sketch = corange_prev + lax.psum(partial_value, ("sx", "sy"))
    return (state, range_sketch, corange_sketch)


def solution(mesh):
    in_specs = (
        P("par", "sx", "sy", None),
        P("par", "sx", "sy", None),
        P(),
        P(None, "sx", "sy", None),
        P("par", "sx", "sy", None),
        P(None, "par"),
    )
    out_specs = (P("par", "sx", "sy", None), P("par", "sx", "sy", None), P(None, "par"))
    return jax.shard_map(
        per_device, mesh=mesh, in_specs=in_specs, out_specs=out_specs, check_vma=False
    )
```

profile of v0, /device:TPU:24, one launch (start us, length us, event | category | flops | bytes accessed | tf_op | source)
XLA Modules:
  0.0 525.8 jit_solution(14510973290693297946)
XLA Ops:
  7.2 0.0 copy-start
  7.2 0.0 all-gather.2.cloned.1.call-start
  7.2 4.8 copy.22
  12.0 3.4 collective-permute-start.2
  15.5 0.0 copy-start.1
  15.5 6.3 %collective-permute-start = (f32[32,1,16,128]{3,0,2,1:T(8,128)S(1)}, f32[32,1,16,128]{3,0,2,1:T(8,128)S(1)}, u32[]{:S(2)}, u32[]{:S(2)}) collective-permute-start(f32[32,1,16,128]{3,0,2,1:T(8,128)S(1)} %get-tuple-element.31), channel_id=1, source_target_pairs={{16,0},{32,16},{48,32},{64,48},{80,64},{96,80},{112,96},{17,1},{33... | collective-permute-start | bytes 786440 | tf_op jit(solution)/shard_map/ppermute | solution.py:17
  21.8 2.4 copy.44
  24.3 1.9 collective-permute-start.3
  26.2 7.5 %collective-permute-start.1 = (f32[32,1,16,128]{3,0,2,1:T(8,128)S(1)}, f32[32,1,16,128]{3,0,2,1:T(8,128)S(1)}, u32[]{:S(2)}, u32[]{:S(2)}) collective-permute-start(f32[32,1,16,128]{3,0,2,1:T(8,128)S(1)} %get-tuple-element.32), channel_id=1, source_target_pairs={{16,0},{32,16},{48,32},{64,48},{80,64},{96,80},{112,96},{17,1},{33... | collective-permute-start | bytes 786440 | tf_op jit(solution)/shard_map/ppermute | solution.py:17
  33.8 0.0 collective-permute-done.2
  33.8 2.4 constant_dynamic-update-slice_fusion.1
  36.2 0.0 collective-permute-done
  36.3 1.3 collective-permute-start.4
  37.6 3.0 collective-permute-start.6
  40.7 0.0 collective-permute-done.3
  40.7 0.7 constant_dynamic-update-slice_fusion.5
  41.4 4.4 constant_dynamic-update-slice_fusion.4
  45.8 0.0 collective-permute-done.1
  45.8 0.7 constant_dynamic-update-slice_fusion.3
  46.5 1.1 fusion.103
  47.6 1.3 collective-permute-start.5
  48.9 4.3 collective-permute-start.7
  53.2 0.0 collective-permute-done.4
  53.2 0.0 collective-permute-done.5
  53.2 1.0 collective-permute-done.7
  54.2 10.3 %fusion.9 = f32[32,16,16,128]{3,0,2,1:T(8,128)S(1)} fusion(f32[32,16,16,128]{3,0,2,1:T(8,128)S(1)} %copy.44, f32[32,18,16,128]{3,0,2,1:T(8,128)} %constant_dynamic-update-slice_fusion.3, f32[32,18,1,128]{3,0,2,1:T(8,128)S(1)} %collective-permute-done.7, f32[32,18,1,128]{3,0,2,1:T(8,128)S(1)} %collective-permute-done.5, ...), kind=kLoop, calls=%fused_computation.19 | loop fusion | flops 40894464 | bytes 24248320 | tf_op jit(solution)/shard_map/add | solution.py:41
  64.5 1.9 collective-permute-start.8
  66.5 3.9 collective-permute-start.9
  70.4 2.4 collective-permute-done.8
  72.8 5.5 %collective-permute-done.9 = f32[32,1,16,128]{3,0,2,1:T(8,128)S(1)} collective-permute-done((f32[32,1,16,128]{3,0,2,1:T(8,128)S(1)}, f32[32,1,16,128]{3,0,2,1:T(8,128)S(1)}, u32[]{:S(2)}, u32[]{:S(2)}) %collective-permute-start.9) | collective-permute-done | bytes 262176 | tf_op jit(solution)/shard_map/ppermute | solution.py:14
  78.4 1.3 collective-permute-start.10
  79.7 5.6 %collective-permute-start.11 = (f32[32,18,1,128]{3,0,2,1:T(8,128)S(1)}, f32[32,18,1,128]{3,0,2,1:T(8,128)S(1)}, u32[]{:S(2)}, u32[]{:S(2)}) collective-permute-start(f32[32,18,1,128]{3,0,2,1:T(8,128)S(1)} %get-tuple-element.19), channel_id=1, source_target_pairs={{0,2},{2,4},{4,6},{6,8},{8,10},{10,12},{12,14},{1,3},{3,5},{5,7},{... | collective-permute-start | bytes 884744 | tf_op jit(solution)/shard_map/ppermute | solution.py:14
  85.3 0.0 collective-permute-done.10
  85.3 1.2 collective-permute-done.11
  86.5 8.1 %fusion.17 = f32[32,16,16,128]{3,0,2,1:T(8,128)S(1)} fusion(f32[32,16,16,128]{3,0,2,1:T(8,128)S(1)} %fusion.9, f32[32,18,1,128]{3,0,2,1:T(8,128)S(1)} %collective-permute-done.11, f32[32,1,16,128]{3,0,2,1:T(8,128)S(1)} %collective-permute-done.8, f32[32,1,16,128]{3,0,2,1:T(8,128)S(1)} %collective-permute-done.9, ...), kind=kLoop, calls=%fused_computation.27 | loop fusion | flops 45088768 | bytes 19529728 | tf_op jit(solution)/shard_map/add | solution.py:41
  94.6 1.9 collective-permute-start.12
  96.5 3.9 collective-permute-start.13
  100.5 2.4 collective-permute-done.12
  102.9 5.5 %collective-permute-done.13 = f32[32,1,16,128]{3,0,2,1:T(8,128)S(1)} collective-permute-done((f32[32,1,16,128]{3,0,2,1:T(8,128)S(1)}, f32[32,1,16,128]{3,0,2,1:T(8,128)S(1)}, u32[]{:S(2)}, u32[]{:S(2)}) %collective-permute-start.13) | collective-permute-done | bytes 262176 | tf_op jit(solution)/shard_map/ppermute | solution.py:14
  108.5 1.3 collective-permute-start.14
  109.8 8.9 %collective-permute-start.15 = (f32[32,18,1,128]{3,0,2,1:T(8,128)S(1)}, f32[32,18,1,128]{3,0,2,1:T(8,128)S(1)}, u32[]{:S(2)}, u32[]{:S(2)}) collective-permute-start(f32[32,18,1,128]{3,0,2,1:T(8,128)S(1)} %get-tuple-element.17), channel_id=1, source_target_pairs={{0,2},{2,4},{4,6},{6,8},{8,10},{10,12},{12,14},{1,3},{3,5},{5,7},{... | collective-permute-start | bytes 884744 | tf_op jit(solution)/shard_map/ppermute | solution.py:14
  118.7 1.2 collective-permute-done.15
  119.8 8.1 %fusion.25 = f32[32,16,16,128]{3,0,2,1:T(8,128)S(1)} fusion(f32[32,16,16,128]{3,0,2,1:T(8,128)S(1)} %fusion.17, f32[32,18,1,128]{3,0,2,1:T(8,128)S(1)} %collective-permute-done.15, f32[32,1,16,128]{3,0,2,1:T(8,128)S(1)} %collective-permute-done.12, f32[32,1,16,128]{3,0,2,1:T(8,128)S(1)} %collective-permute-done.13, ...), kind=kLoop, calls=%fused_computation.35 | loop fusion | flops 45088768 | bytes 19529728 | tf_op jit(solution)/shard_map/add | solution.py:41
  128.0 1.9 collective-permute-start.16
  129.9 3.9 collective-permute-start.17
  133.8 2.4 collective-permute-done.16
  136.2 5.5 %collective-permute-done.17 = f32[32,1,16,128]{3,0,2,1:T(8,128)S(1)} collective-permute-done((f32[32,1,16,128]{3,0,2,1:T(8,128)S(1)}, f32[32,1,16,128]{3,0,2,1:T(8,128)S(1)}, u32[]{:S(2)}, u32[]{:S(2)}) %collective-permute-start.17) | collective-permute-done | bytes 262176 | tf_op jit(solution)/shard_map/ppermute | solution.py:14
  141.8 1.3 collective-permute-start.18
  143.1 8.6 %collective-permute-start.19 = (f32[32,18,1,128]{3,0,2,1:T(8,128)S(1)}, f32[32,18,1,128]{3,0,2,1:T(8,128)S(1)}, u32[]{:S(2)}, u32[]{:S(2)}) collective-permute-start(f32[32,18,1,128]{3,0,2,1:T(8,128)S(1)} %get-tuple-element.15), channel_id=1, source_target_pairs={{0,2},{2,4},{4,6},{6,8},{8,10},{10,12},{12,14},{1,3},{3,5},{5,7},{... | collective-permute-start | bytes 884744 | tf_op jit(solution)/shard_map/ppermute | solution.py:14
  151.7 1.2 collective-permute-done.19
  152.9 9.7 %fusion.100 = (bf16[32,16,16,128]{3,0,2,1:T(8,128)(2,1)S(1)}, f32[32,16,16,128]{3,0,2,1:T(8,128)}) fusion(f32[32,16,16,128]{3,0,2,1:T(8,128)S(1)} %fusion.25, f32[32,16,16,128]{3,0,2,1:T(8,128)S(1)} %copy.22, f32[32,1,16,128]{3,0,2,1:T(8,128)S(1)} %collective-permute-done.16, f32[32,1,16,128]{3,0,2,1:T(8,128)S(1)} %collective-permute-done.17, ...), kind=kLoop, calls=%fused_computation.155 | loop fusion | flops 46137344 | bytes 21626880 | tf_op jit(solution)/shard_map/convert_element_type | solution.py:51
  162.6 2.1 copy.47
  164.8 0.0 all-gather.2.cloned.1.call-update
  164.8 0.0 copy-start.5
  164.8 6.8 %copy.50 = f32[32,16,16,128]{3,2,1,0:T(8,128)} copy(f32[32,16,16,128]{3,0,2,1:T(8,128)} %get-tuple-element.13) | data formatting | bytes 8388608
  171.6 3.7 fusion.94
  175.3 330.3 %psum.7 = f32[64,32]{0,1:T(8,128)S(1)} all-reduce(f32[64,32]{0,1:T(8,128)S(1)} %fusion.94), channel_id=1, replica_groups=mesh['sx'=8,'sy'=8,'par'=2] {'sx','sy'}, use_global_device_ids=true, to_apply=%region_0.1 | all-reduce | flops 2048 | bytes 16384 | tf_op jit(solution)/shard_map/psum | solution.py:71
  505.6 0.6 add.161
  506.2 4.9 copy.69
  511.1 0.0 copy-start.3
  511.2 1.2 copy.56
  512.3 0.4 copy-done.3
  512.7 4.1 add_convert_fusion
  516.8 2.1 copy.51
  (22 shorter events, 0.4 us)
Async XLA Ops:
  7.2 505.2 %copy-start = (bf16[64,64]{1,0:T(8,128)(2,1)S(1)}, bf16[64,64]{1,0:T(8,128)(2,1)}, u32[]{:S(2)}) copy-start(bf16[64,64]{1,0:T(8,128)(2,1)} %param.8) | copy-start | bytes 24580
  7.2 499.1 %all-gather.2.cloned.1.call-start = ((), (), s32[]{:S(2)}) async-start(), calls=%async_computation | async-start | bytes 6291456 | tf_op jit(solution)/shard_map/all_gather | solution.py:57
  7.2 14.6 %copy-start.2 = (f32[32,16,16,128]{3,2,1,0:T(8,128)S(1)}, f32[32,16,16,128]{3,2,1,0:T(8,128)}, u32[]{:S(2)}) copy-start(f32[32,16,16,128]{3,2,1,0:T(8,128)} %param.6) | copy-start | bytes 12582916
  12.0 21.7 %collective-permute-start.2 = (f32[32,1,16,128]{3,0,2,1:T(8,128)S(1)}, f32[32,1,16,128]{3,0,2,1:T(8,128)S(1)}, u32[]{:S(2)}, u32[]{:S(2)}) collective-permute-start(f32[32,1,16,128]{3,0,2,1:T(8,128)S(1)} %get-tuple-element.30), channel_id=1, source_target_pairs={{0,16},{16,32},{32,48},{48,64},{64,80},{80,96},{96,112},{1,17},{17... | collective-permute-start | bytes 786440 | tf_op jit(solution)/shard_map/ppermute | solution.py:14
  15.5 18.3 %copy-start.1 = (f32[32,16,16,128]{3,2,1,0:T(8,128)S(1)}, f32[32,16,16,128]{3,2,1,0:T(8,128)}, u32[]{:S(2)}) copy-start(f32[32,16,16,128]{3,2,1,0:T(8,128)} %param.7) | copy-start | bytes 12582916
  15.5 20.8 %collective-permute-start = (f32[32,1,16,128]{3,0,2,1:T(8,128)S(1)}, f32[32,1,16,128]{3,0,2,1:T(8,128)S(1)}, u32[]{:S(2)}, u32[]{:S(2)}) collective-permute-start(f32[32,1,16,128]{3,0,2,1:T(8,128)S(1)} %get-tuple-element.31), channel_id=1, source_target_pairs={{16,0},{32,16},{48,32},{64,48},{80,64},{96,80},{112,96},{17,1},{33... | collective-permute-start | bytes 786440 | tf_op jit(solution)/shard_map/ppermute | solution.py:17
  24.3 16.4 %collective-permute-start.3 = (f32[32,1,16,128]{3,0,2,1:T(8,128)S(1)}, f32[32,1,16,128]{3,0,2,1:T(8,128)S(1)}, u32[]{:S(2)}, u32[]{:S(2)}) collective-permute-start(f32[32,1,16,128]{3,0,2,1:T(8,128)S(1)} %get-tuple-element.33), channel_id=1, source_target_pairs={{0,16},{16,32},{32,48},{48,64},{64,80},{80,96},{96,112},{1,17},{17... | collective-permute-start | bytes 786440 | tf_op jit(solution)/shard_map/ppermute | solution.py:14
  26.2 19.6 %collective-permute-start.1 = (f32[32,1,16,128]{3,0,2,1:T(8,128)S(1)}, f32[32,1,16,128]{3,0,2,1:T(8,128)S(1)}, u32[]{:S(2)}, u32[]{:S(2)}) collective-permute-start(f32[32,1,16,128]{3,0,2,1:T(8,128)S(1)} %get-tuple-element.32), channel_id=1, source_target_pairs={{16,0},{32,16},{48,32},{64,48},{80,64},{96,80},{112,96},{17,1},{33... | collective-permute-start | bytes 786440 | tf_op jit(solution)/shard_map/ppermute | solution.py:17
  36.3 16.9 %collective-permute-start.4 = (f32[32,18,1,128]{3,0,2,1:T(8,128)S(1)}, f32[32,18,1,128]{3,0,2,1:T(8,128)S(1)}, u32[]{:S(2)}, u32[]{:S(2)}) collective-permute-start(f32[32,18,1,128]{3,0,2,1:T(8,128)S(1)} %get-tuple-element.21), channel_id=1, source_target_pairs={{2,0},{4,2},{6,4},{8,6},{10,8},{12,10},{14,12},{3,1},{5,3},{7,5},{... | collective-permute-start | bytes 884744 | tf_op jit(solution)/shard_map/ppermute | solution.py:17
  37.6 15.6 %collective-permute-start.6 = (f32[32,18,1,128]{3,0,2,1:T(8,128)S(1)}, f32[32,18,1,128]{3,0,2,1:T(8,128)S(1)}, u32[]{:S(2)}, u32[]{:S(2)}) collective-permute-start(f32[32,18,1,128]{3,0,2,1:T(8,128)S(1)} %get-tuple-element.20), channel_id=1, source_target_pairs={{0,2},{2,4},{4,6},{6,8},{8,10},{10,12},{12,14},{1,3},{3,5},{5,7},{... | collective-permute-start | bytes 884744 | tf_op jit(solution)/shard_map/ppermute | solution.py:14
  47.6 5.6 %collective-permute-start.5 = (f32[32,18,1,128]{3,0,2,1:T(8,128)S(1)}, f32[32,18,1,128]{3,0,2,1:T(8,128)S(1)}, u32[]{:S(2)}, u32[]{:S(2)}) collective-permute-start(f32[32,18,1,128]{3,0,2,1:T(8,128)S(1)} %get-tuple-element.22), channel_id=1, source_target_pairs={{2,0},{4,2},{6,4},{8,6},{10,8},{12,10},{14,12},{3,1},{5,3},{7,5},{... | collective-permute-start | bytes 884744 | tf_op jit(solution)/shard_map/ppermute | solution.py:17
  48.9 5.3 collective-permute-start.7
  64.5 8.3 %collective-permute-start.8 = (f32[32,1,16,128]{3,0,2,1:T(8,128)S(1)}, f32[32,1,16,128]{3,0,2,1:T(8,128)S(1)}, u32[]{:S(2)}, u32[]{:S(2)}) collective-permute-start(f32[32,1,16,128]{3,0,2,1:T(8,128)S(1)} %get-tuple-element.29), channel_id=1, source_target_pairs={{16,0},{32,16},{48,32},{64,48},{80,64},{96,80},{112,96},{17,1},{33... | collective-permute-start | bytes 786440 | tf_op jit(solution)/shard_map/ppermute | solution.py:17
  66.5 11.9 %collective-permute-start.9 = (f32[32,1,16,128]{3,0,2,1:T(8,128)S(1)}, f32[32,1,16,128]{3,0,2,1:T(8,128)S(1)}, u32[]{:S(2)}, u32[]{:S(2)}) collective-permute-start(f32[32,1,16,128]{3,0,2,1:T(8,128)S(1)} %get-tuple-element.28), channel_id=1, source_target_pairs={{0,16},{16,32},{32,48},{48,64},{64,80},{80,96},{96,112},{1,17},{17... | collective-permute-start | bytes 786440 | tf_op jit(solution)/shard_map/ppermute | solution.py:14
  78.4 6.9 %collective-permute-start.10 = (f32[32,18,1,128]{3,0,2,1:T(8,128)S(1)}, f32[32,18,1,128]{3,0,2,1:T(8,128)S(1)}, u32[]{:S(2)}, u32[]{:S(2)}) collective-permute-start(f32[32,18,1,128]{3,0,2,1:T(8,128)S(1)} %get-tuple-element.18), channel_id=1, source_target_pairs={{2,0},{4,2},{6,4},{8,6},{10,8},{12,10},{14,12},{3,1},{5,3},{7,5},{... | collective-permute-start | bytes 884744 | tf_op jit(solution)/shard_map/ppermute | solution.py:17
  79.7 6.8 %collective-permute-start.11 = (f32[32,18,1,128]{3,0,2,1:T(8,128)S(1)}, f32[32,18,1,128]{3,0,2,1:T(8,128)S(1)}, u32[]{:S(2)}, u32[]{:S(2)}) collective-permute-start(f32[32,18,1,128]{3,0,2,1:T(8,128)S(1)} %get-tuple-element.19), channel_id=1, source_target_pairs={{0,2},{2,4},{4,6},{6,8},{8,10},{10,12},{12,14},{1,3},{3,5},{5,7},{... | collective-permute-start | bytes 884744 | tf_op jit(solution)/shard_map/ppermute | solution.py:14
  94.6 8.3 %collective-permute-start.12 = (f32[32,1,16,128]{3,0,2,1:T(8,128)S(1)}, f32[32,1,16,128]{3,0,2,1:T(8,128)S(1)}, u32[]{:S(2)}, u32[]{:S(2)}) collective-permute-start(f32[32,1,16,128]{3,0,2,1:T(8,128)S(1)} %get-tuple-element.27), channel_id=1, source_target_pairs={{16,0},{32,16},{48,32},{64,48},{80,64},{96,80},{112,96},{17,1},{33... | collective-permute-start | bytes 786440 | tf_op jit(solution)/shard_map/ppermute | solution.py:17
  96.5 11.9 %collective-permute-start.13 = (f32[32,1,16,128]{3,0,2,1:T(8,128)S(1)}, f32[32,1,16,128]{3,0,2,1:T(8,128)S(1)}, u32[]{:S(2)}, u32[]{:S(2)}) collective-permute-start(f32[32,1,16,128]{3,0,2,1:T(8,128)S(1)} %get-tuple-element.26), channel_id=1, source_target_pairs={{0,16},{16,32},{32,48},{48,64},{64,80},{80,96},{96,112},{1,17},{17... | collective-permute-start | bytes 786440 | tf_op jit(solution)/shard_map/ppermute | solution.py:14
  108.5 10.2 %collective-permute-start.14 = (f32[32,18,1,128]{3,0,2,1:T(8,128)S(1)}, f32[32,18,1,128]{3,0,2,1:T(8,128)S(1)}, u32[]{:S(2)}, u32[]{:S(2)}) collective-permute-start(f32[32,18,1,128]{3,0,2,1:T(8,128)S(1)} %get-tuple-element.16), channel_id=1, source_target_pairs={{2,0},{4,2},{6,4},{8,6},{10,8},{12,10},{14,12},{3,1},{5,3},{7,5},{... | collective-permute-start | bytes 884744 | tf_op jit(solution)/shard_map/ppermute | solution.py:17
  109.8 10.1 %collective-permute-start.15 = (f32[32,18,1,128]{3,0,2,1:T(8,128)S(1)}, f32[32,18,1,128]{3,0,2,1:T(8,128)S(1)}, u32[]{:S(2)}, u32[]{:S(2)}) collective-permute-start(f32[32,18,1,128]{3,0,2,1:T(8,128)S(1)} %get-tuple-element.17), channel_id=1, source_target_pairs={{0,2},{2,4},{4,6},{6,8},{8,10},{10,12},{12,14},{1,3},{3,5},{5,7},{... | collective-permute-start | bytes 884744 | tf_op jit(solution)/shard_map/ppermute | solution.py:14
  128.0 8.3 %collective-permute-start.16 = (f32[32,1,16,128]{3,0,2,1:T(8,128)S(1)}, f32[32,1,16,128]{3,0,2,1:T(8,128)S(1)}, u32[]{:S(2)}, u32[]{:S(2)}) collective-permute-start(f32[32,1,16,128]{3,0,2,1:T(8,128)S(1)} %get-tuple-element.25), channel_id=1, source_target_pairs={{16,0},{32,16},{48,32},{64,48},{80,64},{96,80},{112,96},{17,1},{33... | collective-permute-start | bytes 786440 | tf_op jit(solution)/shard_map/ppermute | solution.py:17
  129.9 11.9 %collective-permute-start.17 = (f32[32,1,16,128]{3,0,2,1:T(8,128)S(1)}, f32[32,1,16,128]{3,0,2,1:T(8,128)S(1)}, u32[]{:S(2)}, u32[]{:S(2)}) collective-permute-start(f32[32,1,16,128]{3,0,2,1:T(8,128)S(1)} %get-tuple-element.24), channel_id=1, source_target_pairs={{0,16},{16,32},{32,48},{48,64},{64,80},{80,96},{96,112},{1,17},{17... | collective-permute-start | bytes 786440 | tf_op jit(solution)/shard_map/ppermute | solution.py:14
  141.8 9.9 %collective-permute-start.18 = (f32[32,18,1,128]{3,0,2,1:T(8,128)S(1)}, f32[32,18,1,128]{3,0,2,1:T(8,128)S(1)}, u32[]{:S(2)}, u32[]{:S(2)}) collective-permute-start(f32[32,18,1,128]{3,0,2,1:T(8,128)S(1)} %get-tuple-element.14), channel_id=1, source_target_pairs={{2,0},{4,2},{6,4},{8,6},{10,8},{12,10},{14,12},{3,1},{5,3},{7,5},{... | collective-permute-start | bytes 884744 | tf_op jit(solution)/shard_map/ppermute | solution.py:17
  143.1 9.8 %collective-permute-start.19 = (f32[32,18,1,128]{3,0,2,1:T(8,128)S(1)}, f32[32,18,1,128]{3,0,2,1:T(8,128)S(1)}, u32[]{:S(2)}, u32[]{:S(2)}) collective-permute-start(f32[32,18,1,128]{3,0,2,1:T(8,128)S(1)} %get-tuple-element.15), channel_id=1, source_target_pairs={{0,2},{2,4},{4,6},{6,8},{8,10},{10,12},{12,14},{1,3},{3,5},{5,7},{... | collective-permute-start | bytes 884744 | tf_op jit(solution)/shard_map/ppermute | solution.py:14
  164.8 6.8 %copy-start.5 = (bf16[64,16,16,128]{3,2,1,0:T(8,128)(2,1)S(1)}, bf16[64,16,16,128]{3,2,1,0:T(8,128)(2,1)}, u32[]{:S(2)}) copy-start(bf16[64,16,16,128]{3,2,1,0:T(8,128)(2,1)} %param.9) | copy-start | bytes 12582916
  171.6 334.0 %copy-start.4 = (f32[64,32]{0,1:T(8,128)S(1)}, f32[64,32]{0,1:T(8,128)}, u32[]{:S(2)}) copy-start(f32[64,32]{0,1:T(8,128)} %param.11) | copy-start | bytes 24580
  511.1 1.6 copy-start.3
Sparse Core Ops, SparseCore 0:
  164.9 63.2 all-gather.1
where the time goes:
time: 527 us; the launch traced here: 526 us
  blocking collectives  330 us (63%)
  starting transfers between devices  73.6 us (14%)
  other arithmetic  36.9 us (7%)
  local copies, waits for them, and re-layouts  34.4 us (7%)
  waiting for transfers between devices  28.3 us (5%)
  between operations  14.5 us (3%)
  matrix products  7.84 us (1%)
    psum x1, blocking collectives, per_device(): corange_sketch = corange_prev + lax.psum(partial_value, ('sx', 'sy'))  330 us
    ppermute x10, starting transfers between devices, extended(): lax.ppermute(lax.slice_in_dim(block, block.shape[dim] - width, None, axis...  47.4 us
    unnamed x22, local copies, waits for them, and re-layouts  30.2 us
    add x3, other arithmetic, advance(): return center + 0.16 * total  26.5 us
    ppermute x10, starting transfers between devices, extended(): lax.ppermute(lax.slice_in_dim(block, 0, width, axis=dim), axis, backward)  26.1 us
    ppermute x10, waiting for transfers between devices, extended(): lax.ppermute(lax.slice_in_dim(block, block.shape[dim] - width, None, axis...  21.1 us
  transfers between devices with their start and end apart: 21, of which 10 were waited for; matrix products, arithmetic and copies ran while one was open for 4% of the time, Pallas kernels for 0%

commit v1 on v0

--- a/solution.py
+++ b/solution.py
@@ -68,7 +68,7 @@
     partial_value = lax.dot_general(
         flat_psi, flat_snap, (((1,), (1,)), ((), ())), preferred_element_type=jnp.float32
     )
-    corange_sketch = corange_prev + lax.psum(partial_value, ("sx", "sy"))
+    corange_sketch = corange_prev + lax.psum(lax.psum(partial_value, "sy"), "sx")
     return (state, range_sketch, corange_sketch)
 
 

time: 527 us -> 263 us (0.50)
  blocking collectives: 330 us -> 66.9 us
    psum x1 -> x2, blocking collectives: 330 us -> 66.9 us  [the longest x1 37.4 us: per_device(): lax.psum(lax.psum(partial_value, 'sy'), 'sx')]
  transfers between devices with their start and end apart: 21 -> 21, of which waited for: 10 -> 10; matrix products, arithmetic and copies ran while one was open for 4% -> 9% of each run, Pallas kernels for 0% -> 0%
where the time goes in v1:
time: 263 us; the launch traced here: 262 us
  starting transfers between devices  73.6 us (28%)
  blocking collectives  66.9 us (25%)
  other arithmetic  36.9 us (14%)
  local copies, waits for them, and re-layouts  34.3 us (13%)
  waiting for transfers between devices  28.3 us (11%)
  between operations  14.5 us (6%)
  matrix products  7.84 us (3%)
    ppermute x10, starting transfers between devices, extended(): lax.ppermute(lax.slice_in_dim(block, block.shape[dim] - width, None, axis...  47.4 us
    psum x1, blocking collectives, per_device(): lax.psum(lax.psum(partial_value, 'sy'), 'sx')  37.4 us
    unnamed x22, local copies, waits for them, and re-layouts  30.2 us
    psum x1, blocking collectives, per_device(): lax.psum(partial_value, 'sy')  29.5 us
    add x3, other arithmetic, advance(): return center + 0.16 * total  26.4 us
    ppermute x10, starting transfers between devices, extended(): lax.ppermute(lax.slice_in_dim(block, 0, width, axis=dim), axis, backward)  26.1 us
    ppermute x10, waiting for transfers between devices, extended(): lax.ppermute(lax.slice_in_dim(block, block.shape[dim] - width, None, axis...  21.1 us
    convert_element_type x1, other arithmetic, per_device(): snapshot = state.astype(jnp.bfloat16)  9.72 us
  transfers between devices with their start and end apart: 21, of which 10 were waited for; matrix products, arithmetic and copies ran while one was open for 9% of the time, Pallas kernels for 0%

profile of v1, /device:TPU:24, one launch (start us, length us, event | category | flops | bytes accessed | tf_op | source)
XLA Modules:
  0.0 262.3 jit_solution(9232263928004582092)
XLA Ops:
  7.2 0.0 copy-start
  7.2 0.0 all-gather.2.cloned.1.call-start
  7.2 4.8 %copy.22 = f32[32,16,16,128]{3,0,2,1:T(8,128)S(1)} copy(f32[32,16,16,128]{3,2,1,0:T(8,128)} %param.7) | data formatting | bytes 8388608 | tf_op args[1]
  12.0 3.4 %collective-permute-start.2 = (f32[32,1,16,128]{3,0,2,1:T(8,128)S(1)}, f32[32,1,16,128]{3,0,2,1:T(8,128)S(1)}, u32[]{:S(2)}, u32[]{:S(2)}) collective-permute-start(f32[32,1,16,128]{3,0,2,1:T(8,128)S(1)} %get-tuple-element.30), channel_id=1, source_target_pairs={{0,16},{16,32},{32,48},{48,64},{64,80},{80,96},{96,112},{1,17},{17... | collective-permute-start | bytes 786440 | tf_op jit(solution)/shard_map/ppermute | solution.py:14
  15.5 0.0 copy-start.1
  15.5 6.3 %collective-permute-start = (f32[32,1,16,128]{3,0,2,1:T(8,128)S(1)}, f32[32,1,16,128]{3,0,2,1:T(8,128)S(1)}, u32[]{:S(2)}, u32[]{:S(2)}) collective-permute-start(f32[32,1,16,128]{3,0,2,1:T(8,128)S(1)} %get-tuple-element.31), channel_id=1, source_target_pairs={{16,0},{32,16},{48,32},{64,48},{80,64},{96,80},{112,96},{17,1},{33... | collective-permute-start | bytes 786440 | tf_op jit(solution)/shard_map/ppermute | solution.py:17
  21.8 2.4 copy.44
  24.3 1.9 collective-permute-start.3
  26.2 7.5 %collective-permute-start.1 = (f32[32,1,16,128]{3,0,2,1:T(8,128)S(1)}, f32[32,1,16,128]{3,0,2,1:T(8,128)S(1)}, u32[]{:S(2)}, u32[]{:S(2)}) collective-permute-start(f32[32,1,16,128]{3,0,2,1:T(8,128)S(1)} %get-tuple-element.32), channel_id=1, source_target_pairs={{16,0},{32,16},{48,32},{64,48},{80,64},{96,80},{112,96},{17,1},{33... | collective-permute-start | bytes 786440 | tf_op jit(solution)/shard_map/ppermute | solution.py:17
  33.8 2.4 constant_dynamic-update-slice_fusion.1
  36.2 0.0 collective-permute-done
  36.3 1.3 collective-permute-start.4
  37.6 3.0 %collective-permute-start.6 = (f32[32,18,1,128]{3,0,2,1:T(8,128)S(1)}, f32[32,18,1,128]{3,0,2,1:T(8,128)S(1)}, u32[]{:S(2)}, u32[]{:S(2)}) collective-permute-start(f32[32,18,1,128]{3,0,2,1:T(8,128)S(1)} %get-tuple-element.20), channel_id=1, source_target_pairs={{0,2},{2,4},{4,6},{6,8},{8,10},{10,12},{12,14},{1,3},{3,5},{5,7},{... | collective-permute-start | bytes 884744 | tf_op jit(solution)/shard_map/ppermute | solution.py:14
  40.7 0.0 collective-permute-done.3
  40.7 0.7 constant_dynamic-update-slice_fusion.5
  41.4 4.4 %constant_dynamic-update-slice_fusion.4 = f32[32,18,16,128]{3,0,2,1:T(8,128)} fusion(f32[32,18,16,128]{3,0,2,1:T(8,128)} %constant_dynamic-update-slice_fusion.5, f32[32,16,16,128]{3,2,1,0:T(8,128)S(1)} %copy-done.2), kind=kLoop, calls=%fused_computation.152 | loop fusion | bytes 8388608
  45.8 0.0 collective-permute-done.1
  45.8 0.7 constant_dynamic-update-slice_fusion.3
  46.5 1.1 fusion.103
  47.6 1.3 collective-permute-start.5
  48.9 4.3 %collective-permute-start.7 = (f32[32,18,1,128]{3,0,2,1:T(8,128)S(1)}, f32[32,18,1,128]{3,0,2,1:T(8,128)S(1)}, u32[]{:S(2)}, u32[]{:S(2)}) collective-permute-start(f32[32,18,1,128]{3,0,2,1:T(8,128)S(1)} %get-tuple-element.23), channel_id=1, source_target_pairs={{0,2},{2,4},{4,6},{6,8},{8,10},{10,12},{12,14},{1,3},{3,5},{5,7},{... | collective-permute-start | bytes 884744 | tf_op jit(solution)/shard_map/ppermute | solution.py:14
  53.2 0.0 collective-permute-done.5
  53.2 1.0 collective-permute-done.7
  54.2 10.3 %fusion.9 = f32[32,16,16,128]{3,0,2,1:T(8,128)S(1)} fusion(f32[32,16,16,128]{3,0,2,1:T(8,128)S(1)} %copy.44, f32[32,18,16,128]{3,0,2,1:T(8,128)} %constant_dynamic-update-slice_fusion.3, f32[32,18,1,128]{3,0,2,1:T(8,128)S(1)} %collective-permute-done.7, f32[32,18,1,128]{3,0,2,1:T(8,128)S(1)} %collective-permute-done.5, ...), kind=kLoop, calls=%fused_computation.19 | loop fusion | flops 40894464 | bytes 24248320 | tf_op jit(solution)/shard_map/add | solution.py:41
  64.5 1.9 collective-permute-start.8
  66.4 3.9 %collective-permute-start.9 = (f32[32,1,16,128]{3,0,2,1:T(8,128)S(1)}, f32[32,1,16,128]{3,0,2,1:T(8,128)S(1)}, u32[]{:S(2)}, u32[]{:S(2)}) collective-permute-start(f32[32,1,16,128]{3,0,2,1:T(8,128)S(1)} %get-tuple-element.28), channel_id=1, source_target_pairs={{0,16},{16,32},{32,48},{48,64},{64,80},{80,96},{96,112},{1,17},{17... | collective-permute-start | bytes 786440 | tf_op jit(solution)/shard_map/ppermute | solution.py:14
  70.3 2.4 collective-permute-done.8
  72.7 5.5 %collective-permute-done.9 = f32[32,1,16,128]{3,0,2,1:T(8,128)S(1)} collective-permute-done((f32[32,1,16,128]{3,0,2,1:T(8,128)S(1)}, f32[32,1,16,128]{3,0,2,1:T(8,128)S(1)}, u32[]{:S(2)}, u32[]{:S(2)}) %collective-permute-start.9) | collective-permute-done | bytes 262176 | tf_op jit(solution)/shard_map/ppermute | solution.py:14
  78.3 1.3 collective-permute-start.10
  79.6 5.6 %collective-permute-start.11 = (f32[32,18,1,128]{3,0,2,1:T(8,128)S(1)}, f32[32,18,1,128]{3,0,2,1:T(8,128)S(1)}, u32[]{:S(2)}, u32[]{:S(2)}) collective-permute-start(f32[32,18,1,128]{3,0,2,1:T(8,128)S(1)} %get-tuple-element.19), channel_id=1, source_target_pairs={{0,2},{2,4},{4,6},{6,8},{8,10},{10,12},{12,14},{1,3},{3,5},{5,7},{... | collective-permute-start | bytes 884744 | tf_op jit(solution)/shard_map/ppermute | solution.py:14
  85.2 1.2 collective-permute-done.11
  86.4 8.1 %fusion.17 = f32[32,16,16,128]{3,0,2,1:T(8,128)S(1)} fusion(f32[32,16,16,128]{3,0,2,1:T(8,128)S(1)} %fusion.9, f32[32,18,1,128]{3,0,2,1:T(8,128)S(1)} %collective-permute-done.11, f32[32,1,16,128]{3,0,2,1:T(8,128)S(1)} %collective-permute-done.8, f32[32,1,16,128]{3,0,2,1:T(8,128)S(1)} %collective-permute-done.9, ...), kind=kLoop, calls=%fused_computation.27 | loop fusion | flops 45088768 | bytes 19529728 | tf_op jit(solution)/shard_map/add | solution.py:41
  94.5 1.9 collective-permute-start.12
  96.5 3.9 %collective-permute-start.13 = (f32[32,1,16,128]{3,0,2,1:T(8,128)S(1)}, f32[32,1,16,128]{3,0,2,1:T(8,128)S(1)}, u32[]{:S(2)}, u32[]{:S(2)}) collective-permute-start(f32[32,1,16,128]{3,0,2,1:T(8,128)S(1)} %get-tuple-element.26), channel_id=1, source_target_pairs={{0,16},{16,32},{32,48},{48,64},{64,80},{80,96},{96,112},{1,17},{17... | collective-permute-start | bytes 786440 | tf_op jit(solution)/shard_map/ppermute | solution.py:14
  100.4 2.4 collective-permute-done.12
  102.8 5.5 %collective-permute-done.13 = f32[32,1,16,128]{3,0,2,1:T(8,128)S(1)} collective-permute-done((f32[32,1,16,128]{3,0,2,1:T(8,128)S(1)}, f32[32,1,16,128]{3,0,2,1:T(8,128)S(1)}, u32[]{:S(2)}, u32[]{:S(2)}) %collective-permute-start.13) | collective-permute-done | bytes 262176 | tf_op jit(solution)/shard_map/ppermute | solution.py:14
  108.4 1.3 collective-permute-start.14
  109.7 8.9 %collective-permute-start.15 = (f32[32,18,1,128]{3,0,2,1:T(8,128)S(1)}, f32[32,18,1,128]{3,0,2,1:T(8,128)S(1)}, u32[]{:S(2)}, u32[]{:S(2)}) collective-permute-start(f32[32,18,1,128]{3,0,2,1:T(8,128)S(1)} %get-tuple-element.17), channel_id=1, source_target_pairs={{0,2},{2,4},{4,6},{6,8},{8,10},{10,12},{12,14},{1,3},{3,5},{5,7},{... | collective-permute-start | bytes 884744 | tf_op jit(solution)/shard_map/ppermute | solution.py:14
  118.6 0.0 collective-permute-done.14
  118.6 1.2 collective-permute-done.15
  119.8 8.1 %fusion.25 = f32[32,16,16,128]{3,0,2,1:T(8,128)S(1)} fusion(f32[32,16,16,128]{3,0,2,1:T(8,128)S(1)} %fusion.17, f32[32,18,1,128]{3,0,2,1:T(8,128)S(1)} %collective-permute-done.15, f32[32,1,16,128]{3,0,2,1:T(8,128)S(1)} %collective-permute-done.12, f32[32,1,16,128]{3,0,2,1:T(8,128)S(1)} %collective-permute-done.13, ...), kind=kLoop, calls=%fused_computation.35 | loop fusion | flops 45088768 | bytes 19529728 | tf_op jit(solution)/shard_map/add | solution.py:41
  127.9 1.9 collective-permute-start.16
  129.8 3.9 %collective-permute-start.17 = (f32[32,1,16,128]{3,0,2,1:T(8,128)S(1)}, f32[32,1,16,128]{3,0,2,1:T(8,128)S(1)}, u32[]{:S(2)}, u32[]{:S(2)}) collective-permute-start(f32[32,1,16,128]{3,0,2,1:T(8,128)S(1)} %get-tuple-element.24), channel_id=1, source_target_pairs={{0,16},{16,32},{32,48},{48,64},{64,80},{80,96},{96,112},{1,17},{17... | collective-permute-start | bytes 786440 | tf_op jit(solution)/shard_map/ppermute | solution.py:14
  133.8 2.4 collective-permute-done.16
  136.2 5.5 %collective-permute-done.17 = f32[32,1,16,128]{3,0,2,1:T(8,128)S(1)} collective-permute-done((f32[32,1,16,128]{3,0,2,1:T(8,128)S(1)}, f32[32,1,16,128]{3,0,2,1:T(8,128)S(1)}, u32[]{:S(2)}, u32[]{:S(2)}) %collective-permute-start.17) | collective-permute-done | bytes 262176 | tf_op jit(solution)/shard_map/ppermute | solution.py:14
  141.8 1.3 collective-permute-start.18
  143.1 8.6 %collective-permute-start.19 = (f32[32,18,1,128]{3,0,2,1:T(8,128)S(1)}, f32[32,18,1,128]{3,0,2,1:T(8,128)S(1)}, u32[]{:S(2)}, u32[]{:S(2)}) collective-permute-start(f32[32,18,1,128]{3,0,2,1:T(8,128)S(1)} %get-tuple-element.15), channel_id=1, source_target_pairs={{0,2},{2,4},{4,6},{6,8},{8,10},{10,12},{12,14},{1,3},{3,5},{5,7},{... | collective-permute-start | bytes 884744 | tf_op jit(solution)/shard_map/ppermute | solution.py:14
  151.7 0.0 collective-permute-done.18
  151.7 1.2 collective-permute-done.19
  152.8 9.7 %fusion.100 = (bf16[32,16,16,128]{3,0,2,1:T(8,128)(2,1)S(1)}, f32[32,16,16,128]{3,0,2,1:T(8,128)}) fusion(f32[32,16,16,128]{3,0,2,1:T(8,128)S(1)} %fusion.25, f32[32,16,16,128]{3,0,2,1:T(8,128)S(1)} %copy.22, f32[32,1,16,128]{3,0,2,1:T(8,128)S(1)} %collective-permute-done.16, f32[32,1,16,128]{3,0,2,1:T(8,128)S(1)} %collective-permute-done.17, ...), kind=kLoop, calls=%fused_computation.155 | loop fusion | flops 46137344 | bytes 21626880 | tf_op jit(solution)/shard_map/convert_element_type | solution.py:51
  162.6 2.1 copy.47
  164.7 0.0 all-gather.2.cloned.1.call-update
  164.7 0.0 copy-start.5
  164.7 6.8 %copy.50 = f32[32,16,16,128]{3,2,1,0:T(8,128)} copy(f32[32,16,16,128]{3,0,2,1:T(8,128)} %get-tuple-element.13) | data formatting | bytes 8388608
  171.5 3.7 %fusion.94 = f32[64,32]{0,1:T(8,128)S(1)} fusion(bf16[32,16,16,128]{3,0,2,1:T(8,128)(2,1)S(1)} %get-tuple-element.12, bf16[64,16,16,128]{3,2,1,0:T(8,128)(2,1)S(1)} %copy-done.5), kind=kOutput, calls=%fused_computation.136 | convolution fusion | flops 134217728 | bytes 6299648 | tf_op jit(solution)/shard_map/dot_general | solution.py:68
  175.3 29.5 %psum.14 = f32[64,32]{0,1:T(8,128)S(1)} all-reduce(f32[64,32]{0,1:T(8,128)S(1)} %fusion.94), channel_id=1, replica_groups=mesh['sx'=8,'sy'=8,'par'=2] {'sy'}, use_global_device_ids=true, to_apply=%region_0.1 | all-reduce | flops 2048 | bytes 16384 | tf_op jit(solution)/shard_map/psum | solution.py:71
  204.8 37.4 %psum.15 = f32[64,32]{0,1:T(8,128)S(1)} all-reduce(f32[64,32]{0,1:T(8,128)S(1)} %psum.14), channel_id=1, replica_groups=mesh['sx'=8,'sy'=8,'par'=2] {'sx'}, use_global_device_ids=true, to_apply=%region_1.2 | all-reduce | flops 2048 | bytes 16384 | tf_op jit(solution)/shard_map/psum | solution.py:71
  242.2 0.6 add.163
  242.8 4.9 %copy.69 = bf16[8,8,256,128]{3,1,2,0:T(8,128)(2,1)S(1)} copy(bf16[8,8,256,128]{3,2,1,0:T(8,128)(2,1)} %bitcast.27) | data formatting | bytes 8388608
  247.7 0.0 copy-start.3
  247.7 1.2 copy.56
  248.9 0.4 copy-done.3
  249.3 4.1 %add_convert_fusion = bf16[32,16,16,128]{3,0,2,1:T(8,128)(2,1)S(1)} fusion(bf16[16,16,128,64]{2,1,0,3:T(8,128)(2,1)S(1)} %bitcast.26, bf16[32,16,16,128]{3,2,1,0:T(8,128)(2,1)S(1)} %copy-done.3, bf16[64,64]{1,0:T(8,128)(2,1)S(1)} %copy-done, s32[]{:T(128)S(6)} %select_n.3), kind=kOutput, calls=%fused_computation.135 | convolution fusion | flops 137363456 | bytes 8396804 | tf_op jit(solution)/shard_map/dot_general | solution.py:59
  253.4 2.1 copy.51
  (23 shorter events, 0.4 us)
Async XLA Ops:
  7.2 241.7 %copy-start = (bf16[64,64]{1,0:T(8,128)(2,1)S(1)}, bf16[64,64]{1,0:T(8,128)(2,1)}, u32[]{:S(2)}) copy-start(bf16[64,64]{1,0:T(8,128)(2,1)} %param.8) | copy-start | bytes 24580
  7.2 235.6 %all-gather.2.cloned.1.call-start = ((), (), s32[]{:S(2)}) async-start(), calls=%async_computation | async-start | bytes 6291456 | tf_op jit(solution)/shard_map/all_gather | solution.py:57
  7.2 14.6 %copy-start.2 = (f32[32,16,16,128]{3,2,1,0:T(8,128)S(1)}, f32[32,16,16,128]{3,2,1,0:T(8,128)}, u32[]{:S(2)}) copy-start(f32[32,16,16,128]{3,2,1,0:T(8,128)} %param.6) | copy-start | bytes 12582916
  12.0 21.7 %collective-permute-start.2 = (f32[32,1,16,128]{3,0,2,1:T(8,128)S(1)}, f32[32,1,16,128]{3,0,2,1:T(8,128)S(1)}, u32[]{:S(2)}, u32[]{:S(2)}) collective-permute-start(f32[32,1,16,128]{3,0,2,1:T(8,128)S(1)} %get-tuple-element.30), channel_id=1, source_target_pairs={{0,16},{16,32},{32,48},{48,64},{64,80},{80,96},{96,112},{1,17},{17... | collective-permute-start | bytes 786440 | tf_op jit(solution)/shard_map/ppermute | solution.py:14
  15.5 18.3 %copy-start.1 = (f32[32,16,16,128]{3,2,1,0:T(8,128)S(1)}, f32[32,16,16,128]{3,2,1,0:T(8,128)}, u32[]{:S(2)}) copy-start(f32[32,16,16,128]{3,2,1,0:T(8,128)} %param.7) | copy-start | bytes 12582916
  15.5 20.8 %collective-permute-start = (f32[32,1,16,128]{3,0,2,1:T(8,128)S(1)}, f32[32,1,16,128]{3,0,2,1:T(8,128)S(1)}, u32[]{:S(2)}, u32[]{:S(2)}) collective-permute-start(f32[32,1,16,128]{3,0,2,1:T(8,128)S(1)} %get-tuple-element.31), channel_id=1, source_target_pairs={{16,0},{32,16},{48,32},{64,48},{80,64},{96,80},{112,96},{17,1},{33... | collective-permute-start | bytes 786440 | tf_op jit(solution)/shard_map/ppermute | solution.py:17
  24.3 16.4 %collective-permute-start.3 = (f32[32,1,16,128]{3,0,2,1:T(8,128)S(1)}, f32[32,1,16,128]{3,0,2,1:T(8,128)S(1)}, u32[]{:S(2)}, u32[]{:S(2)}) collective-permute-start(f32[32,1,16,128]{3,0,2,1:T(8,128)S(1)} %get-tuple-element.33), channel_id=1, source_target_pairs={{0,16},{16,32},{32,48},{48,64},{64,80},{80,96},{96,112},{1,17},{17... | collective-permute-start | bytes 786440 | tf_op jit(solution)/shard_map/ppermute | solution.py:14
  26.2 19.6 %collective-permute-start.1 = (f32[32,1,16,128]{3,0,2,1:T(8,128)S(1)}, f32[32,1,16,128]{3,0,2,1:T(8,128)S(1)}, u32[]{:S(2)}, u32[]{:S(2)}) collective-permute-start(f32[32,1,16,128]{3,0,2,1:T(8,128)S(1)} %get-tuple-element.32), channel_id=1, source_target_pairs={{16,0},{32,16},{48,32},{64,48},{80,64},{96,80},{112,96},{17,1},{33... | collective-permute-start | bytes 786440 | tf_op jit(solution)/shard_map/ppermute | solution.py:17
  36.3 16.8 %collective-permute-start.4 = (f32[32,18,1,128]{3,0,2,1:T(8,128)S(1)}, f32[32,18,1,128]{3,0,2,1:T(8,128)S(1)}, u32[]{:S(2)}, u32[]{:S(2)}) collective-permute-start(f32[32,18,1,128]{3,0,2,1:T(8,128)S(1)} %get-tuple-element.21), channel_id=1, source_target_pairs={{2,0},{4,2},{6,4},{8,6},{10,8},{12,10},{14,12},{3,1},{5,3},{7,5},{... | collective-permute-start | bytes 884744 | tf_op jit(solution)/shard_map/ppermute | solution.py:17
  37.6 15.6 %collective-permute-start.6 = (f32[32,18,1,128]{3,0,2,1:T(8,128)S(1)}, f32[32,18,1,128]{3,0,2,1:T(8,128)S(1)}, u32[]{:S(2)}, u32[]{:S(2)}) collective-permute-start(f32[32,18,1,128]{3,0,2,1:T(8,128)S(1)} %get-tuple-element.20), channel_id=1, source_target_pairs={{0,2},{2,4},{4,6},{6,8},{8,10},{10,12},{12,14},{1,3},{3,5},{5,7},{... | collective-permute-start | bytes 884744 | tf_op jit(solution)/shard_map/ppermute | solution.py:14
  47.6 5.6 %collective-permute-start.5 = (f32[32,18,1,128]{3,0,2,1:T(8,128)S(1)}, f32[32,18,1,128]{3,0,2,1:T(8,128)S(1)}, u32[]{:S(2)}, u32[]{:S(2)}) collective-permute-start(f32[32,18,1,128]{3,0,2,1:T(8,128)S(1)} %get-tuple-element.22), channel_id=1, source_target_pairs={{2,0},{4,2},{6,4},{8,6},{10,8},{12,10},{14,12},{3,1},{5,3},{7,5},{... | collective-permute-start | bytes 884744 | tf_op jit(solution)/shard_map/ppermute | solution.py:17
  48.9 5.3 %collective-permute-start.7 = (f32[32,18,1,128]{3,0,2,1:T(8,128)S(1)}, f32[32,18,1,128]{3,0,2,1:T(8,128)S(1)}, u32[]{:S(2)}, u32[]{:S(2)}) collective-permute-start(f32[32,18,1,128]{3,0,2,1:T(8,128)S(1)} %get-tuple-element.23), channel_id=1, source_target_pairs={{0,2},{2,4},{4,6},{6,8},{8,10},{10,12},{12,14},{1,3},{3,5},{5,7},{... | collective-permute-start | bytes 884744 | tf_op jit(solution)/shard_map/ppermute | solution.py:14
  64.5 8.3 %collective-permute-start.8 = (f32[32,1,16,128]{3,0,2,1:T(8,128)S(1)}, f32[32,1,16,128]{3,0,2,1:T(8,128)S(1)}, u32[]{:S(2)}, u32[]{:S(2)}) collective-permute-start(f32[32,1,16,128]{3,0,2,1:T(8,128)S(1)} %get-tuple-element.29), channel_id=1, source_target_pairs={{16,0},{32,16},{48,32},{64,48},{80,64},{96,80},{112,96},{17,1},{33... | collective-permute-start | bytes 786440 | tf_op jit(solution)/shard_map/ppermute | solution.py:17
  66.4 11.9 %collective-permute-start.9 = (f32[32,1,16,128]{3,0,2,1:T(8,128)S(1)}, f32[32,1,16,128]{3,0,2,1:T(8,128)S(1)}, u32[]{:S(2)}, u32[]{:S(2)}) collective-permute-start(f32[32,1,16,128]{3,0,2,1:T(8,128)S(1)} %get-tuple-element.28), channel_id=1, source_target_pairs={{0,16},{16,32},{32,48},{48,64},{64,80},{80,96},{96,112},{1,17},{17... | collective-permute-start | bytes 786440 | tf_op jit(solution)/shard_map/ppermute | solution.py:14
  78.3 6.9 %collective-permute-start.10 = (f32[32,18,1,128]{3,0,2,1:T(8,128)S(1)}, f32[32,18,1,128]{3,0,2,1:T(8,128)S(1)}, u32[]{:S(2)}, u32[]{:S(2)}) collective-permute-start(f32[32,18,1,128]{3,0,2,1:T(8,128)S(1)} %get-tuple-element.18), channel_id=1, source_target_pairs={{2,0},{4,2},{6,4},{8,6},{10,8},{12,10},{14,12},{3,1},{5,3},{7,5},{... | collective-permute-start | bytes 884744 | tf_op jit(solution)/shard_map/ppermute | solution.py:17
  79.6 6.8 %collective-permute-start.11 = (f32[32,18,1,128]{3,0,2,1:T(8,128)S(1)}, f32[32,18,1,128]{3,0,2,1:T(8,128)S(1)}, u32[]{:S(2)}, u32[]{:S(2)}) collective-permute-start(f32[32,18,1,128]{3,0,2,1:T(8,128)S(1)} %get-tuple-element.19), channel_id=1, source_target_pairs={{0,2},{2,4},{4,6},{6,8},{8,10},{10,12},{12,14},{1,3},{3,5},{5,7},{... | collective-permute-start | bytes 884744 | tf_op jit(solution)/shard_map/ppermute | solution.py:14
  94.5 8.3 %collective-permute-start.12 = (f32[32,1,16,128]{3,0,2,1:T(8,128)S(1)}, f32[32,1,16,128]{3,0,2,1:T(8,128)S(1)}, u32[]{:S(2)}, u32[]{:S(2)}) collective-permute-start(f32[32,1,16,128]{3,0,2,1:T(8,128)S(1)} %get-tuple-element.27), channel_id=1, source_target_pairs={{16,0},{32,16},{48,32},{64,48},{80,64},{96,80},{112,96},{17,1},{33... | collective-permute-start | bytes 786440 | tf_op jit(solution)/shard_map/ppermute | solution.py:17
  96.5 11.9 %collective-permute-start.13 = (f32[32,1,16,128]{3,0,2,1:T(8,128)S(1)}, f32[32,1,16,128]{3,0,2,1:T(8,128)S(1)}, u32[]{:S(2)}, u32[]{:S(2)}) collective-permute-start(f32[32,1,16,128]{3,0,2,1:T(8,128)S(1)} %get-tuple-element.26), channel_id=1, source_target_pairs={{0,16},{16,32},{32,48},{48,64},{64,80},{80,96},{96,112},{1,17},{17... | collective-permute-start | bytes 786440 | tf_op jit(solution)/shard_map/ppermute | solution.py:14
  108.4 10.2 %collective-permute-start.14 = (f32[32,18,1,128]{3,0,2,1:T(8,128)S(1)}, f32[32,18,1,128]{3,0,2,1:T(8,128)S(1)}, u32[]{:S(2)}, u32[]{:S(2)}) collective-permute-start(f32[32,18,1,128]{3,0,2,1:T(8,128)S(1)} %get-tuple-element.16), channel_id=1, source_target_pairs={{2,0},{4,2},{6,4},{8,6},{10,8},{12,10},{14,12},{3,1},{5,3},{7,5},{... | collective-permute-start | bytes 884744 | tf_op jit(solution)/shard_map/ppermute | solution.py:17
  109.7 10.1 %collective-permute-start.15 = (f32[32,18,1,128]{3,0,2,1:T(8,128)S(1)}, f32[32,18,1,128]{3,0,2,1:T(8,128)S(1)}, u32[]{:S(2)}, u32[]{:S(2)}) collective-permute-start(f32[32,18,1,128]{3,0,2,1:T(8,128)S(1)} %get-tuple-element.17), channel_id=1, source_target_pairs={{0,2},{2,4},{4,6},{6,8},{8,10},{10,12},{12,14},{1,3},{3,5},{5,7},{... | collective-permute-start | bytes 884744 | tf_op jit(solution)/shard_map/ppermute | solution.py:14
  127.9 8.3 %collective-permute-start.16 = (f32[32,1,16,128]{3,0,2,1:T(8,128)S(1)}, f32[32,1,16,128]{3,0,2,1:T(8,128)S(1)}, u32[]{:S(2)}, u32[]{:S(2)}) collective-permute-start(f32[32,1,16,128]{3,0,2,1:T(8,128)S(1)} %get-tuple-element.25), channel_id=1, source_target_pairs={{16,0},{32,16},{48,32},{64,48},{80,64},{96,80},{112,96},{17,1},{33... | collective-permute-start | bytes 786440 | tf_op jit(solution)/shard_map/ppermute | solution.py:17
  129.8 11.9 %collective-permute-start.17 = (f32[32,1,16,128]{3,0,2,1:T(8,128)S(1)}, f32[32,1,16,128]{3,0,2,1:T(8,128)S(1)}, u32[]{:S(2)}, u32[]{:S(2)}) collective-permute-start(f32[32,1,16,128]{3,0,2,1:T(8,128)S(1)} %get-tuple-element.24), channel_id=1, source_target_pairs={{0,16},{16,32},{32,48},{48,64},{64,80},{80,96},{96,112},{1,17},{17... | collective-permute-start | bytes 786440 | tf_op jit(solution)/shard_map/ppermute | solution.py:14
  141.8 9.9 %collective-permute-start.18 = (f32[32,18,1,128]{3,0,2,1:T(8,128)S(1)}, f32[32,18,1,128]{3,0,2,1:T(8,128)S(1)}, u32[]{:S(2)}, u32[]{:S(2)}) collective-permute-start(f32[32,18,1,128]{3,0,2,1:T(8,128)S(1)} %get-tuple-element.14), channel_id=1, source_target_pairs={{2,0},{4,2},{6,4},{8,6},{10,8},{12,10},{14,12},{3,1},{5,3},{7,5},{... | collective-permute-start | bytes 884744 | tf_op jit(solution)/shard_map/ppermute | solution.py:17
  143.1 9.8 %collective-permute-start.19 = (f32[32,18,1,128]{3,0,2,1:T(8,128)S(1)}, f32[32,18,1,128]{3,0,2,1:T(8,128)S(1)}, u32[]{:S(2)}, u32[]{:S(2)}) collective-permute-start(f32[32,18,1,128]{3,0,2,1:T(8,128)S(1)} %get-tuple-element.15), channel_id=1, source_target_pairs={{0,2},{2,4},{4,6},{6,8},{8,10},{10,12},{12,14},{1,3},{3,5},{5,7},{... | collective-permute-start | bytes 884744 | tf_op jit(solution)/shard_map/ppermute | solution.py:14
  164.7 6.8 %copy-start.5 = (bf16[64,16,16,128]{3,2,1,0:T(8,128)(2,1)S(1)}, bf16[64,16,16,128]{3,2,1,0:T(8,128)(2,1)}, u32[]{:S(2)}) copy-start(bf16[64,16,16,128]{3,2,1,0:T(8,128)(2,1)} %param.9) | copy-start | bytes 12582916
  171.5 70.6 %copy-start.4 = (f32[64,32]{0,1:T(8,128)S(1)}, f32[64,32]{0,1:T(8,128)}, u32[]{:S(2)}) copy-start(f32[64,32]{0,1:T(8,128)} %param.11) | copy-start | bytes 24580
  247.7 1.6 copy-start.3
Sparse Core Ops, SparseCore 0:
  164.8 63.8 all-gather.1
